TPU v7x, 32 devices: a whole 2x2x4 slice. The times are simulated.
32 devices in a mesh: wide: 16 (over z, y, x), narrow: 2 (over core).
Axes of the slice: x: 2, y: 2, z: 4, core: 2. Of those that a mesh axis runs over, the one named last changes fastest.
Arguments:
- passages: bfloat16 [16384, 768], P('wide'), may hold values from -32 to 32
- centroids: bfloat16 [4096, 768], P('narrow'), may hold values from -6 to 6
Outputs:
- new_centroids: float32 [4096, 768], P('narrow')
- row_potential: float32 [16384], P('wide')
- col_potential: float32 [4096], P('narrow')
All inputs are finite; a program needn't handle non-finite values.
Results may differ from a plain program's by a relative error of at most 0.00035.
Values sent between devices are 32-bit elements; how exact they have to be, the bound alone decides.
A program may use at most 64 MiB of HBM per device.

v0:
```python
import jax
import jax.numpy as jnp
from jax import lax
from jax.sharding import PartitionSpec as P

VECTOR_DIMENSION = 768
CENTROIDS = 4096
SWEEPS = 3


entropic_regularizer = 0.02


def inverse_rms(values):
    wide_values = values.astype(jnp.float32)
    return lax.rsqrt(jnp.mean(wide_values * wide_values, axis=1) + 1e-06)


def unit_rows(totals):
    return totals * lax.rsqrt(jnp.mean(totals * totals, axis=1, keepdims=True) + 1e-06)


def body(passages, centroids):
    passage_row_scale = inverse_rms(passages)
    cluster_center_factor = inverse_rms(centroids)
    cosine_affinity_matrix = lax.dot_general(
        passages, centroids, (((1,), (1,)), ((), ())), preferred_element_type=jnp.float32
    )
    kernel = jnp.exp(
        cosine_affinity_matrix
        * passage_row_scale[:, None]
        * cluster_center_factor[None, :]
        * (1.0 / (VECTOR_DIMENSION * entropic_regularizer))
    )
    target = float(lax.axis_size("wide") * passages.shape[0]) / float(
        lax.axis_size("narrow") * centroids.shape[0]
    )
    col_factor = jnp.ones((centroids.shape[0],), jnp.float32)
    row_factor = jnp.ones((passages.shape[0],), jnp.float32)
    for number in range(SWEEPS):
        row_part = jnp.dot(kernel, col_factor, precision=lax.Precision.HIGHEST)
        row_factor = 1.0 / lax.psum(row_part, "narrow")
        col_part = jnp.dot(row_factor, kernel, precision=lax.Precision.HIGHEST)
        col_factor = target / lax.psum(col_part, "wide")
    weights = (
        row_factor[:, None] * kernel * col_factor[None, :] * passage_row_scale[:, None]
    ).astype(jnp.bfloat16)
    partial_sums = lax.dot_general(
        weights, passages, (((0,), (0,)), ((), ())), preferred_element_type=jnp.float32
    )
    new_centroids = unit_rows(lax.psum(partial_sums, "wide"))
    row_potential = jnp.log(CENTROIDS * row_factor)
    return (new_centroids, row_potential, jnp.log(col_factor))


def solution(mesh):
    in_specs = (P("wide", None), P("narrow", None))
    out_specs = (P("narrow", None), P("wide"), P("narrow"))
    return jax.shard_map(body, mesh=mesh, in_specs=in_specs, out_specs=out_specs, check_vma=False)
```

profile of v0, /device:TPU:0, one launch (start us, length us, event | category | flops | bytes accessed | tf_op | source)
XLA Modules:
  0.0 426.3 jit_solution(12740581471887425097)
XLA Ops:
  7.2 0.0 all-reduce.2.cloned.1.call-start
  7.2 1.8 multiply_reduce_fusion.2
  9.0 2.6 multiply_reduce_fusion.1
  11.6 6.0 %multiply_exponential_fusion = f32[1024,2048]{1,0:T(8,128)S(1)} fusion(bf16[1024,768]{1,0:T(8,128)(2,1)} %param.2, bf16[2048,768]{1,0:T(8,128)(2,1)} %param.3, f32[2048]{0:T(1024)S(1)} %add_rsqrt_fusion.1, f32[1024]{0:T(1024)S(1)} %add_rsqrt_fusion.2), kind=kOutput, calls=%fused_computation.1 | convolution fusion | flops 3227516928 | bytes 13119488 | tf_op jit(solution)/shard_map/dot_general | solution.py:26
  17.6 0.0 copy-start
  17.6 3.2 copy-done
  20.8 7.1 %fusion.4 = f32[1,1024]{1,0:T(1,128)S(1)} fusion(f32[1024,2048]{1,0:T(8,128)S(1)} %multiply_exponential_fusion), kind=kOutput, calls=%fused_computation.12 | convolution fusion | flops 25165824 | bytes 8392704 | tf_op jit(solution)/shard_map/dot_general | solution.py:41
  28.0 2.6 psum.49
  30.6 6.3 %fusion.8 = f32[1,2048]{1,0:T(1,128)S(1)} fusion(f32[1024,1]{0,1:T(1,128)S(1)} %bitcast.31, f32[1024,2048]{1,0:T(8,128)} %copy-done), kind=kOutput, calls=%fused_computation.24 | convolution fusion | flops 25165824 | bytes 8400896 | tf_op jit(solution)/shard_map/dot_general | solution.py:43
  36.9 44.0 %psum.50 = f32[2048]{0:T(1024)S(1)} all-reduce(f32[2048]{0:T(1024)S(1)} %bitcast.25), channel_id=1, replica_groups=mesh['wide'=16,'narrow'=2] {'wide'}, use_global_device_ids=true, to_apply=%region_3.0 | all-reduce | flops 2048 | bytes 16384 | tf_op jit(solution)/shard_map/psum | solution.py:44
  81.0 9.4 %fusion.9 = f32[1,1024]{1,0:T(1,128)S(1)} fusion(f32[1024,2048]{1,0:T(8,128)} %copy-done, f32[2048,1]{0,1:T(1,128)S(1)} %bitcast.26), kind=kOutput, calls=%fused_computation.25 | convolution fusion | flops 25165824 | bytes 8400896 | tf_op jit(solution)/shard_map/dot_general | solution.py:41
  90.4 2.5 psum.51
  92.9 6.3 %fusion.10 = f32[1,2048]{1,0:T(1,128)S(1)} fusion(f32[1024,1]{0,1:T(1,128)S(1)} %bitcast.33, f32[1024,2048]{1,0:T(8,128)} %copy-done), kind=kOutput, calls=%fused_computation.26 | convolution fusion | flops 25165824 | bytes 8400896 | tf_op jit(solution)/shard_map/dot_general | solution.py:43
  99.2 37.1 %psum.52 = f32[2048]{0:T(1024)S(1)} all-reduce(f32[2048]{0:T(1024)S(1)} %bitcast.27), channel_id=1, replica_groups=mesh['wide'=16,'narrow'=2] {'wide'}, use_global_device_ids=true, to_apply=%region_5.0 | all-reduce | flops 2048 | bytes 16384 | tf_op jit(solution)/shard_map/psum | solution.py:44
  136.3 0.0 copy-start.2
  136.3 9.5 %fusion.11 = f32[1,1024]{1,0:T(1,128)S(1)} fusion(f32[1024,2048]{1,0:T(8,128)} %copy-done, f32[2048,1]{0,1:T(1,128)S(1)} %bitcast.28), kind=kOutput, calls=%fused_computation.27 | convolution fusion | flops 25165824 | bytes 8400896 | tf_op jit(solution)/shard_map/dot_general | solution.py:41
  145.8 2.5 psum.53
  148.3 0.6 multiply_log_fusion
  148.9 6.3 %fusion.12 = f32[1,2048]{1,0:T(1,128)S(1)} fusion(f32[1024,1]{0,1:T(1,128)S(1)} %bitcast.30, f32[1024,2048]{1,0:T(8,128)} %copy-done), kind=kOutput, calls=%fused_computation.28 | convolution fusion | flops 25165824 | bytes 8400896 | tf_op jit(solution)/shard_map/dot_general | solution.py:43
  155.2 39.3 %psum.54 = f32[2048]{0:T(1024)S(1)} all-reduce(f32[2048]{0:T(1024)S(1)} %bitcast.29), channel_id=1, replica_groups=mesh['wide'=16,'narrow'=2] {'wide'}, use_global_device_ids=true, to_apply=%region_7.0 | all-reduce | flops 2048 | bytes 16384 | tf_op jit(solution)/shard_map/psum | solution.py:44
  194.6 0.6 fusion.7
  195.2 0.0 copy-done.2
  195.2 10.1 %fusion = f32[2048,768]{1,0:T(8,128)} fusion(bf16[1024,768]{1,0:T(8,128)(2,1)S(1)} %copy-done.2, f32[1024,2048]{1,0:T(8,128)} %copy-done, f32[2048]{0:T(1024)S(1)} %get-tuple-element.4, f32[1024]{0:T(1024)S(1)} %get-tuple-element.6, f32[1024]{0:T(1024)S(1)} %add_rsqrt_fusion.2), kind=kOutput, calls=%fused_computation.4 | convolution fusion | flops 3229614080 | bytes 16269312 | tf_op jit(solution)/shard_map/dot_general | solution.py:48
  205.3 0.0 all-reduce.2.cloned.1.call-update
  205.3 206.4 %all-reduce.2.cloned.1.call-done = f32[2048,768]{1,0:T(8,128)} async-done(((f32[2048,768]{1,0:T(8,128)}), f32[2048,768]{1,0:T(8,128)}) %all-reduce.2.cloned.1.call-update) | async-done | bytes 6291472 | tf_op jit(solution)/shard_map/psum | solution.py:51
  411.7 0.0 copy-start.1
  411.7 3.4 multiply_reduce_fusion
  415.1 1.2 copy-done.1
  416.3 3.2 broadcast_multiply_fusion
  (7 shorter events, 0.0 us)
Async XLA Ops:
  7.2 404.5 %all-reduce.2.cloned.1.call-start = ((), (), s32[]{:S(2)}) async-start(), calls=%async_computation | async-start | bytes 12582912 | tf_op jit(solution)/shard_map/psum | solution.py:51
  17.6 3.2 copy-start
  136.3 58.9 %copy-start.2 = (bf16[1024,768]{1,0:T(8,128)(2,1)S(1)}, bf16[1024,768]{1,0:T(8,128)(2,1)}, u32[]{:S(2)}) copy-start(bf16[1024,768]{1,0:T(8,128)(2,1)} %param.2) | copy-start | bytes 4718596
  411.7 4.6 %copy-start.1 = (f32[2048,768]{1,0:T(8,128)S(1)}, f32[2048,768]{1,0:T(8,128)}, u32[]{:S(2)}) copy-start(f32[2048,768]{1,0:T(8,128)} %all-reduce.2.cloned.1.call-done) | copy-start | bytes 18874372
Sparse Core Ops, SparseCore 0:
  205.4 206.2 all-reduce.1
where the time goes:
time: 427 us; the launch traced here: 426 us
  waiting for transfers between devices  206 us (48%)
  blocking collectives  128 us (30%)
  matrix products  61.2 us (14%)
  between operations  14.1 us (3%)
  other arithmetic  12.2 us (3%)
  local copies, waits for them, and re-layouts  4.39 us (1%)
    psum x1, waiting for transfers between devices, body(): new_centroids = unit_rows(lax.psum(partial_sums, 'wide'))  206 us
    psum x3, blocking collectives, body(): col_factor = target / lax.psum(col_part, 'wide')  120 us
    dot_general x3, matrix products, body(): row_part = jnp.dot(kernel, col_factor, precision=lax.Precision.HIGHEST)  26 us
    dot_general x3, matrix products, body(): col_part = jnp.dot(row_factor, kernel, precision=lax.Precision.HIGHEST)  19 us
    dot_general x1, matrix products, body(): lax.dot_general(weights, passages, (((0,), (0,)), ((), ())), preferred_el...  10.1 us
  transfers between devices with their start and end apart: 1, of which 1 were waited for; matrix products, arithmetic and copies ran while one was open for 0% of the time, Pallas kernels for 0%

commit v1 on v0

v1 whole, which is shorter than its diff:
```python
import functools

import jax
import jax.numpy as jnp
from jax import lax
from jax.experimental import pallas as pl
from jax.experimental.pallas import tpu as pltpu
from jax.sharding import PartitionSpec as P

VECTOR_DIMENSION = 768
CENTROIDS = 4096
SWEEPS = 3
LANES = 128
CHUNKS = 4
MESH = pl.DeviceIdType.MESH

entropic_regularizer = 0.02
LOG2_E = 1.4426950408889634


def unit_rows(totals):
    return totals * lax.rsqrt(jnp.mean(totals * totals, axis=1, keepdims=True) + 1e-06)


def lane_groups(values):
    total = values[:, :LANES]
    for start in range(LANES, values.shape[1], LANES):
        total = total + values[:, start : start + LANES]
    return total


def to_lanes(values):
    ones = jnp.ones((8, LANES), jnp.float32)
    sums = lax.dot_general(
        ones, values, (((1,), (1,)), ((), ())),
        precision=lax.Precision.HIGHEST, preferred_element_type=jnp.float32,
    )
    return sums[0:1, :]


def kernel(
    n_wide, n_narrow, reduce_here,
    p_ref, c_ref, out_ref, rowpot_ref, colpot_ref,
    k_ref, scale_ref, cent_ref, col_ref, row_ref,
    rows_ref, mass_ref, rows_send, rows_recv, mass_send, mass_recv, *reduce_refs,
):
    m, n = k_ref.shape
    wide, narrow = lax.axis_index("wide"), lax.axis_index("narrow")

    barrier = pltpu.get_barrier_semaphore()

    def greet_wide(step, carry):
        pl.semaphore_signal(
            barrier, inc=1, device_id={"wide": lax.rem(wide + step, n_wide)}, device_id_type=MESH
        )
        return carry

    def greet_narrow(step, carry):
        pl.semaphore_signal(
            barrier, inc=1, device_id={"narrow": lax.rem(narrow + step, n_narrow)}, device_id_type=MESH
        )
        return carry

    lax.fori_loop(1, n_wide, greet_wide, 0)
    lax.fori_loop(1, n_narrow, greet_narrow, 0)

    cb = 256
    for j in range(n // cb):
        values = c_ref[j * cb : (j + 1) * cb, :].astype(jnp.float32)
        squares = to_lanes(lane_groups(values * values))
        cent_ref[:, j * cb : (j + 1) * cb] = lax.rsqrt(
            squares * (1.0 / VECTOR_DIMENSION) + 1e-06
        ) * (LOG2_E / (VECTOR_DIMENSION * entropic_regularizer))

    bm, bn = 256, 512

    @pl.loop(0, m // bm)
    def _(i):
        at = pl.ds(pl.multiple_of(i * bm, bm), bm)
        block = p_ref[at, :]
        values = block.astype(jnp.float32)
        scale = lax.rsqrt(
            jnp.sum(lane_groups(values * values), axis=1, keepdims=True) * (1.0 / VECTOR_DIMENSION) + 1e-06
        )
        scale_ref[at, :] = jnp.broadcast_to(scale, (bm, LANES))
        total = jnp.zeros((bm, LANES), jnp.float32)
        for j in range(n // bn):
            cols = slice(j * bn, (j + 1) * bn)
            scores = lax.dot_general(
                block, c_ref[cols, :], (((1,), (1,)), ((), ())), preferred_element_type=jnp.float32
            )
            entries = jnp.exp2(scores * scale * cent_ref[:, cols])
            k_ref[at, cols] = entries
            total = total + lane_groups(entries)
        rows_ref[0, pl.ds(narrow, 1), :, at] = to_lanes(total)[None]

    pl.semaphore_wait(barrier, n_wide - 1 + n_narrow - 1)

    target = float(n_wide * m) / float(n_narrow * n)
    rb = 128

    def exchange(sweep, buffer, axis, me, size, send, recv):
        def copy(peer, slot):
            return pltpu.make_async_remote_copy(
                src_ref=buffer.at[sweep, slot],
                dst_ref=buffer.at[sweep, slot],
                send_sem=send.at[sweep, peer],
                recv_sem=recv.at[sweep, slot],
                device_id={axis: peer},
                device_id_type=MESH,
            )

        def start(step, carry):
            copy(lax.rem(me + step, size), me).start()
            return carry

        def arrive(step, carry):
            peer = lax.rem(me + step, size)
            copy(peer, peer).wait_recv()
            return carry

        def sent(step, carry):
            copy(lax.rem(me + step, size), me).wait_send()
            return carry

        lax.fori_loop(1, size, start, 0)
        lax.fori_loop(1, size, arrive, 0)
        lax.fori_loop(1, size, sent, 0)
        total = buffer[sweep, 0]
        for slot in range(1, size):
            total = total + buffer[sweep, slot]
        return total

    for sweep in range(SWEEPS):
        if sweep > 0:

            @pl.loop(0, m // rb)
            def _(i):
                at = pl.ds(pl.multiple_of(i * rb, rb), rb)
                total = jnp.zeros((rb, LANES), jnp.float32)
                for t in range(n // LANES):
                    cols = slice(t * LANES, (t + 1) * LANES)
                    total = total + k_ref[at, cols] * col_ref[:, cols]
                rows_ref[sweep, pl.ds(narrow, 1), :, at] = to_lanes(total)[None]

        row_factor = 1.0 / exchange(sweep, rows_ref, "narrow", narrow, n_narrow, rows_send, rows_recv)
        row_ref[...] = row_factor

        last = sweep == SWEEPS - 1

        def mass_step(i, partial):
            at = pl.ds(pl.multiple_of(i * rb, rb), rb)
            factor = jnp.transpose(jnp.broadcast_to(row_ref[:, at], (LANES, rb)))
            if last:
                scale_ref[at, :] = scale_ref[at, :] * factor
            sums = []
            for t in range(n // LANES):
                cols = slice(t * LANES, (t + 1) * LANES)
                product = k_ref[at, cols] * factor
                sums.append(partial[t] + jnp.sum(product.reshape(rb // 8, 8, LANES), axis=0))
            return tuple(sums)

        zeros = tuple(jnp.zeros((8, LANES), jnp.float32) for _ in range(n // LANES))
        sums = lax.fori_loop(0, m // rb, mass_step, zeros)
        for t in range(n // LANES):
            mass_ref[sweep, pl.ds(wide, 1), :, t * LANES : (t + 1) * LANES] = jnp.sum(
                sums[t], axis=0, keepdims=True
            )[None]
        if last:
            rowpot_ref[...] = jnp.log(CENTROIDS * row_factor)
        col_ref[...] = target / exchange(sweep, mass_ref, "wide", wide, n_wide, mass_send, mass_recv)

    colpot_ref[...] = jnp.log(col_ref[...])

    tb = 128

    def totals_block(into, start):
        cols = pl.ds(pl.multiple_of(start, tb), tb)
        weights = (k_ref[:, cols] * scale_ref[...] * col_ref[:, cols]).astype(jnp.bfloat16)
        into[cols, :] = lax.dot_general(
            weights, p_ref[...], (((0,), (0,)), ((), ())), preferred_element_type=jnp.float32
        )

    if not reduce_here:

        @pl.loop(0, n // tb)
        def _(j):
            totals_block(out_ref, j * tb)

        return

    t_ref, got1, got2, got3, s1, r1, s2, r2, s3, r3, s4, r4, s5, r5, s6, r6 = reduce_refs
    line = n_wide // 4
    half = n // 2
    r = half // CHUNKS
    z, y, x = wide // 4, lax.rem(wide // 2, 2), lax.rem(wide, 2)
    over_x = z * 4 + y * 2 + (1 - x)
    over_y = z * 4 + (1 - y) * 2 + x
    partners = ((over_x, over_y), (over_y, over_x))
    bits = ((x, y), (y, x))
    plane = lax.rem(wide, 4)

    def rows_of(start, size):
        return pl.ds(pl.multiple_of(start, 8), size)

    def remote(src, dst, send, recv, peer):
        return pltpu.make_async_remote_copy(
            src_ref=src, dst_ref=dst, send_sem=send, recv_sem=recv,
            device_id={"wide": peer}, device_id_type=MESH,
        )

    def base(h, k):
        return h * half + k * r

    def my_half(h, k):
        return base(h, k) + bits[h][0] * (r // 2)

    def other_half(h, k):
        return base(h, k) + (1 - bits[h][0]) * (r // 2)

    def my_quarter(h, k):
        return my_half(h, k) + bits[h][1] * (r // 4)

    def other_quarter(h, k):
        return my_half(h, k) + (1 - bits[h][1]) * (r // 4)

    shard = r // 4 // line

    def first(h, k):
        return remote(
            t_ref.at[rows_of(other_half(h, k), r // 2)], got1.at[h, k],
            s1.at[h, k], r1.at[h, k], partners[h][0],
        )

    def second(h, k):
        return remote(
            t_ref.at[rows_of(other_quarter(h, k), r // 4)], got2.at[h, k],
            s2.at[h, k], r2.at[h, k], partners[h][1],
        )

    def third(h, k, peer, slot):
        return remote(
            t_ref.at[rows_of(my_quarter(h, k) + peer * shard, shard)], got3.at[h, k, slot],
            s3.at[h, k, peer], r3.at[h, k, slot], peer * 4 + plane,
        )

    def fourth(h, k, peer, slot):
        piece = rows_of(my_quarter(h, k) + slot * shard, shard)
        return remote(
            out_ref.at[piece], out_ref.at[piece],
            s4.at[h, k, peer], r4.at[h, k, slot], peer * 4 + plane,
        )

    def fifth(h, k, start):
        piece = rows_of(start, r // 4)
        return remote(
            out_ref.at[piece], out_ref.at[piece], s5.at[h, k], r5.at[h, k], partners[h][1]
        )

    def sixth(h, k, start):
        piece = rows_of(start, r // 2)
        return remote(
            out_ref.at[piece], out_ref.at[piece], s6.at[h, k], r6.at[h, k], partners[h][0]
        )

    def others(action):
        for step in range(1, line):
            action(lax.rem(z + step, line))

    pairs = [(h, k) for k in range(CHUNKS) for h in range(2)]

    for h, k in pairs:

        @pl.loop(0, r // tb)
        def _(j):
            totals_block(t_ref, base(h, k) + j * tb)

        first(h, k).start()

    for h, k in pairs:
        first(h, k).wait_recv()
        for q in range(2):
            sends = other_quarter(h, k) if q == 0 else my_quarter(h, k)
            at = rows_of(sends, r // 4)
            t_ref[at, :] = t_ref[at, :] + got1[h, k, rows_of(sends - my_half(h, k), r // 4), :]
            if q == 0:
                second(h, k).start()

    def after_second(h, k):
        second(h, k).wait_recv()
        at = rows_of(my_quarter(h, k), r // 4)
        t_ref[at, :] = t_ref[at, :] + got2[h, k]
        others(lambda peer: third(h, k, peer, z).start())

    def after_third(h, k):
        others(lambda peer: third(h, k, z, peer).wait_recv())
        at = rows_of(my_quarter(h, k) + z * shard, shard)
        total = t_ref[at, :]
        for step in range(1, line):
            total = total + got3[h, k, lax.rem(z + step, line)]
        out_ref[at, :] = unit_rows(total)
        others(lambda peer: fourth(h, k, peer, z).start())

    def after_fourth(h, k):
        others(lambda peer: fourth(h, k, z, peer).wait_recv())
        fifth(h, k, my_quarter(h, k)).start()

    stages = (after_second, after_third, after_fourth)
    for step in range(len(pairs) + 4):
        for number, stage in enumerate(stages):
            index = step - 2 * number
            if 0 <= index < len(pairs):
                stage(*pairs[index])
    for h, k in pairs:
        fifth(h, k, other_quarter(h, k)).wait_recv()
        sixth(h, k, my_half(h, k)).start()
    for h, k in pairs:
        sixth(h, k, other_half(h, k)).wait_recv()
    for h, k in pairs:
        first(h, k).wait_send()
        second(h, k).wait_send()
        others(lambda peer: third(h, k, peer, z).wait_send())
        others(lambda peer: fourth(h, k, peer, z).wait_send())
        fifth(h, k, my_quarter(h, k)).wait_send()
        sixth(h, k, my_half(h, k)).wait_send()


def solution(mesh):
    n_wide, n_narrow = mesh.shape["wide"], mesh.shape["narrow"]

    def body(passages, centroids):
        m, d = passages.shape
        n = centroids.shape[0]
        reduce_here = n_wide % 4 == 0 and n % (8 * 2 * CHUNKS * n_wide) == 0
        dma = pltpu.SemaphoreType.DMA
        scratch = [
            pltpu.VMEM((m, n), jnp.float32),
            pltpu.VMEM((m, LANES), jnp.float32),
            pltpu.VMEM((1, n), jnp.float32),
            pltpu.VMEM((1, n), jnp.float32),
            pltpu.VMEM((1, m), jnp.float32),
            pltpu.VMEM((SWEEPS, n_narrow, 1, m), jnp.float32),
            pltpu.VMEM((SWEEPS, n_wide, 1, n), jnp.float32),
            dma((SWEEPS, n_narrow)),
            dma((SWEEPS, n_narrow)),
            dma((SWEEPS, n_wide)),
            dma((SWEEPS, n_wide)),
        ]
        if reduce_here:
            r = n // 2 // CHUNKS
            line = n_wide // 4
            scratch += [
                pltpu.VMEM((n, d), jnp.float32),
                pltpu.VMEM((2, CHUNKS, r // 2, d), jnp.float32),
                pltpu.VMEM((2, CHUNKS, r // 4, d), jnp.float32),
                pltpu.VMEM((2, CHUNKS, line, r // 4 // line, d), jnp.float32),
            ]
            pair, lines = dma((2, CHUNKS)), dma((2, CHUNKS, line))
            scratch += [pair] * 4 + [lines] * 4 + [pair] * 4
        vmem = pl.BlockSpec(memory_space=pltpu.VMEM)
        totals, row_potential, col_potential = pl.pallas_call(
            functools.partial(kernel, n_wide, n_narrow, reduce_here),
            out_shape=(
                jax.ShapeDtypeStruct((n, d), jnp.float32),
                jax.ShapeDtypeStruct((1, m), jnp.float32),
                jax.ShapeDtypeStruct((1, n), jnp.float32),
            ),
            in_specs=[vmem, vmem],
            out_specs=(vmem, vmem, vmem),
            scratch_shapes=scratch,
            compiler_params=pltpu.CompilerParams(collective_id=0, has_side_effects=True),
        )(passages, centroids)
        if not reduce_here:
            totals = unit_rows(lax.psum(totals, "wide"))
        return totals, row_potential.reshape(m), col_potential.reshape(n)

    in_specs = (P("wide", None), P("narrow", None))
    out_specs = (P("narrow", None), P("wide"), P("narrow"))
    return jax.shard_map(body, mesh=mesh, in_specs=in_specs, out_specs=out_specs, check_vma=False)
```

time: 427 us -> 201 us (0.47)
  waiting for transfers between devices: 206 us -> 0 us
  Pallas kernels: 0 us -> 194 us
  blocking collectives: 128 us -> 0 us
  matrix products: 61.2 us -> 0 us
  between operations: 14.1 us -> 0.66 us
  other arithmetic: 12.2 us -> 0 us
    psum x1 -> x0, waiting for transfers between devices: 206 us -> none  [body(): new_centroids = unit_rows(lax.psum(partial_sums, 'wide'))]
    pallas_call x0 -> x1, Pallas kernels: none -> 194 us  [body(): pl.pallas_call(functools.partial(kernel, n_wide, n_narrow, reduce_here),...]
    psum x6 -> x0, blocking collectives: 128 us -> none  [the longest x3 120 us: body(): col_factor = target / lax.psum(col_part, 'wide')]
    dot_general x8 -> x0, matrix products: 61.2 us -> none  [the longest x3 26 us: body(): row_part = jnp.dot(kernel, col_factor, precision=lax.Precision.HIGHEST)]
    reduce_sum x3 -> x0, other arithmetic: 7.77 us -> none  [the longest x2 4.36 us: inverse_rms(): return lax.rsqrt(jnp.mean(wide_values * wide_values, axis=1) + 1e-06)]
  transfers between devices with their start and end apart: 1 -> 0, of which waited for: 1 -> 0; matrix products, arithmetic and copies ran while one was open for 0% -> 0% of each run, Pallas kernels for 0% -> 0%
where the time goes in v1:
time: 201 us
  Pallas kernels  194 us (97%)
  local copies, waits for them, and re-layouts  7.1 us (4%)
    pallas_call x1, Pallas kernels, body(): pl.pallas_call(functools.partial(kernel, n_wide, n_narrow, reduce_here),...  194 us
    unnamed x7, local copies, waits for them, and re-layouts  7.1 us

profile of v1, /device:TPU:0, one launch (start us, length us, event | category | flops | bytes accessed | tf_op | source)
XLA Modules:
  0.0 201.3 jit_solution(1364508294641858038)
XLA Ops:
  0.6 193.6 %shard_map.49 = (f32[2048,768]{1,0:T(8,128)}, f32[1,1024]{1,0:T(1,128)}, f32[1,2048]{1,0:T(1,128)}) custom-call(bf16[1024,768]{1,0:T(8,128)(2,1)} %p_ref.1, bf16[2048,768]{1,0:T(8,128)(2,1)} %c_ref.1), custom_call_target="tpu_custom_call" | custom-call | tf_op jit(solution)/shard_map/pallas_call | solution.py:361
  194.2 0.0 copy-start.1
  194.2 0.0 copy-start
  194.2 5.9 %copy.8 = f32[2048,768]{1,0:T(8,128)} copy(f32[2048,768]{1,0:T(8,128)} %get-tuple-element.12) | data formatting | bytes 12582912
  200.1 0.0 copy-done.1
  200.1 0.6 copy.9
  200.7 0.0 copy-done
  200.7 0.6 copy.10
Async XLA Ops:
  194.2 5.9 %copy-start.1 = (f32[1,1024]{1,0:T(1,128)S(1)}, f32[1,1024]{1,0:T(1,128)}, u32[]{:S(2)}) copy-start(f32[1,1024]{1,0:T(1,128)} %get-tuple-element.7) | copy-start | bytes 12292
  194.2 6.5 %copy-start = (f32[1,2048]{1,0:T(1,128)S(1)}, f32[1,2048]{1,0:T(1,128)}, u32[]{:S(2)}) copy-start(f32[1,2048]{1,0:T(1,128)} %get-tuple-element.8) | copy-start | bytes 24580

commit v2 on v1

--- a/solution.py
+++ b/solution.py
@@ -1,4 +1,5 @@
 import functools
+import heapq
 
 import jax
 import jax.numpy as jnp
@@ -11,11 +12,45 @@
 CENTROIDS = 4096
 SWEEPS = 3
 LANES = 128
-CHUNKS = 4
+CHUNKS = 8
+AHEAD = 2
+VMEM_LIMIT = 38 * 1024 * 1024
 MESH = pl.DeviceIdType.MESH
 
 entropic_regularizer = 0.02
 LOG2_E = 1.4426950408889634
+
+
+def plan(chunks):
+    pairs = [(half, chunk) for chunk in range(chunks) for half in range(2)]
+    sizes = (0.5, 0.25, 0.25, 0.25, 0.25, 0.5)
+    free = {"x": 0.0, "y": 0.0, "z": 0.0}
+    events, order, issued = [], [], 0
+    unit = 512.0 / chunks * 0.132
+
+    def send(at, pair, stage):
+        axes = ("x", "y") if pair[0] == 0 else ("y", "x")
+        link = (axes[0], axes[1], "z", "z", axes[1], axes[0])[stage]
+        free[link] = max(at, free[link]) + sizes[stage] * unit
+        heapq.heappush(events, (free[link] + (3.4 if link == "z" else 1.8), len(order), pair, stage))
+
+    clock = 0.0
+    while issued < min(2 * AHEAD, len(pairs)):
+        clock += 3.6 / chunks
+        send(clock, pairs[issued], 0)
+        issued += 1
+    while events:
+        at, _, pair, stage = heapq.heappop(events)
+        clock = max(clock, at) + (2.8, 1.6, 1.2, 0.1, 0.1, 0.1)[stage] / chunks
+        follows = stage == 0 and issued < len(pairs)
+        order.append((pair, stage, pairs[issued] if follows else None))
+        if stage < 5:
+            send(clock, pair, stage + 1)
+        if follows:
+            clock += 3.6 / chunks
+            send(clock, pairs[issued], 0)
+            issued += 1
+    return order
 
 
 def unit_rows(totals):
@@ -269,22 +304,22 @@
 
     pairs = [(h, k) for k in range(CHUNKS) for h in range(2)]
 
-    for h, k in pairs:
-
+    def begin(h, k):
         @pl.loop(0, r // tb)
         def _(j):
             totals_block(t_ref, base(h, k) + j * tb)
 
         first(h, k).start()
 
-    for h, k in pairs:
+    def add_first(h, k, quarter):
+        at = rows_of(quarter, r // 4)
+        t_ref[at, :] = t_ref[at, :] + got1[h, k, rows_of(quarter - my_half(h, k), r // 4), :]
+
+    def after_first(h, k):
         first(h, k).wait_recv()
-        for q in range(2):
-            sends = other_quarter(h, k) if q == 0 else my_quarter(h, k)
-            at = rows_of(sends, r // 4)
-            t_ref[at, :] = t_ref[at, :] + got1[h, k, rows_of(sends - my_half(h, k), r // 4), :]
-            if q == 0:
-                second(h, k).start()
+        add_first(h, k, other_quarter(h, k))
+        second(h, k).start()
+        add_first(h, k, my_quarter(h, k))
 
     def after_second(h, k):
         second(h, k).wait_recv()
@@ -305,17 +340,20 @@
         others(lambda peer: fourth(h, k, z, peer).wait_recv())
         fifth(h, k, my_quarter(h, k)).start()
 
-    stages = (after_second, after_third, after_fourth)
-    for step in range(len(pairs) + 4):
-        for number, stage in enumerate(stages):
-            index = step - 2 * number
-            if 0 <= index < len(pairs):
-                stage(*pairs[index])
-    for h, k in pairs:
+    def after_fifth(h, k):
         fifth(h, k, other_quarter(h, k)).wait_recv()
         sixth(h, k, my_half(h, k)).start()
-    for h, k in pairs:
+
+    def after_sixth(h, k):
         sixth(h, k, other_half(h, k)).wait_recv()
+
+    stages = (after_first, after_second, after_third, after_fourth, after_fifth, after_sixth)
+    for pair in pairs[: 2 * AHEAD]:
+        begin(*pair)
+    for pair, stage, following in plan(CHUNKS):
+        stages[stage](*pair)
+        if following is not None:
+            begin(*following)
     for h, k in pairs:
         first(h, k).wait_send()
         second(h, k).wait_send()
@@ -368,7 +406,9 @@
             in_specs=[vmem, vmem],
             out_specs=(vmem, vmem, vmem),
             scratch_shapes=scratch,
-            compiler_params=pltpu.CompilerParams(collective_id=0, has_side_effects=True),
+            compiler_params=pltpu.CompilerParams(
+                collective_id=0, has_side_effects=True, vmem_limit_bytes=VMEM_LIMIT
+            ),
         )(passages, centroids)
         if not reduce_here:
             totals = unit_rows(lax.psum(totals, "wide"))

time: 201 us -> 154 us (0.77)
  Pallas kernels: 194 us -> 146 us
    pallas_call x1, Pallas kernels: 194 us -> 146 us  [body(): pl.pallas_call(functools.partial(kernel, n_wide, n_narrow, reduce_here),...]
where the time goes in v2:
time: 154 us; the launch traced here: 153 us
  Pallas kernels  146 us (95%)
  local copies, waits for them, and re-layouts  7.19 us (5%)
    pallas_call x1, Pallas kernels, body(): pl.pallas_call(functools.partial(kernel, n_wide, n_narrow, reduce_here),...  146 us
    unnamed x7, local copies, waits for them, and re-layouts  7.19 us

profile of v2, /device:TPU:0, one launch (start us, length us, event | category | flops | bytes accessed | tf_op | source)
XLA Modules:
  0.0 153.4 jit_solution(600770044386227705)
XLA Ops:
  0.6 0.0 copy-start
  0.6 1.9 %copy-done = bf16[2048,768]{1,0:T(8,128)(2,1)S(1)} copy-done((bf16[2048,768]{1,0:T(8,128)(2,1)S(1)}, bf16[2048,768]{1,0:T(8,128)(2,1)}, u32[]{:S(2)}) %copy-start) | copy-done | bytes 3145752
  2.5 0.0 copy-start.1
  2.5 1.4 copy-done.1
  3.9 145.6 %shard_map.49 = (f32[2048,768]{1,0:T(8,128)S(1)}, f32[1,1024]{1,0:T(1,128)S(1)}, f32[1,2048]{1,0:T(1,128)S(1)}) custom-call(bf16[1024,768]{1,0:T(8,128)(2,1)S(1)} %copy-done.1, bf16[2048,768]{1,0:T(8,128)(2,1)S(1)} %copy-done), custom_call_target="tpu_custom_call" | custom-call | tf_op jit(solution)/shard_map/pallas_call | solution.py:399
  149.5 2.7 %copy.8 = f32[2048,768]{1,0:T(8,128)} copy(f32[2048,768]{1,0:T(8,128)S(1)} %get-tuple-element.12) | data formatting | bytes 12582912
  152.2 0.6 copy.9
  152.8 0.6 copy.10
Async XLA Ops:
  0.6 1.9 %copy-start = (bf16[2048,768]{1,0:T(8,128)(2,1)S(1)}, bf16[2048,768]{1,0:T(8,128)(2,1)}, u32[]{:S(2)}) copy-start(bf16[2048,768]{1,0:T(8,128)(2,1)} %c_ref.1) | copy-start | bytes 9437188
  2.5 1.4 copy-start.1

commit v3 on v2

--- a/solution.py
+++ b/solution.py
@@ -132,7 +132,7 @@
     pl.semaphore_wait(barrier, n_wide - 1 + n_narrow - 1)
 
     target = float(n_wide * m) / float(n_narrow * n)
-    rb = 128
+    rb, wb = 128, 256
 
     def exchange(sweep, buffer, axis, me, size, send, recv):
         def copy(peer, slot):
@@ -169,10 +169,10 @@
     for sweep in range(SWEEPS):
         if sweep > 0:
 
-            @pl.loop(0, m // rb)
+            @pl.loop(0, m // wb)
             def _(i):
-                at = pl.ds(pl.multiple_of(i * rb, rb), rb)
-                total = jnp.zeros((rb, LANES), jnp.float32)
+                at = pl.ds(pl.multiple_of(i * wb, wb), wb)
+                total = jnp.zeros((wb, LANES), jnp.float32)
                 for t in range(n // LANES):
                     cols = slice(t * LANES, (t + 1) * LANES)
                     total = total + k_ref[at, cols] * col_ref[:, cols]

time: 154 us -> 152 us (0.987)
  Pallas kernels: 146 us -> 144 us
where the time goes in v3:
time: 152 us
  Pallas kernels  144 us (95%)
  local copies, waits for them, and re-layouts  7.19 us (5%)
    pallas_call x1, Pallas kernels, body(): pl.pallas_call(functools.partial(kernel, n_wide, n_narrow, reduce_here),...  144 us
    unnamed x7, local copies, waits for them, and re-layouts  7.19 us

profile of v3, /device:TPU:0, one launch (start us, length us, event | category | flops | bytes accessed | tf_op | source)
XLA Modules:
  0.0 152.0 jit_solution(11660884074115402914)
XLA Ops:
  0.6 0.0 copy-start
  0.6 1.9 %copy-done = bf16[2048,768]{1,0:T(8,128)(2,1)S(1)} copy-done((bf16[2048,768]{1,0:T(8,128)(2,1)S(1)}, bf16[2048,768]{1,0:T(8,128)(2,1)}, u32[]{:S(2)}) %copy-start) | copy-done | bytes 3145752
  2.5 0.0 copy-start.1
  2.5 1.4 copy-done.1
  3.9 144.2 %shard_map.49 = (f32[2048,768]{1,0:T(8,128)S(1)}, f32[1,1024]{1,0:T(1,128)S(1)}, f32[1,2048]{1,0:T(1,128)S(1)}) custom-call(bf16[1024,768]{1,0:T(8,128)(2,1)S(1)} %copy-done.1, bf16[2048,768]{1,0:T(8,128)(2,1)S(1)} %copy-done), custom_call_target="tpu_custom_call" | custom-call | tf_op jit(solution)/shard_map/pallas_call | solution.py:399
  148.1 2.7 %copy.8 = f32[2048,768]{1,0:T(8,128)} copy(f32[2048,768]{1,0:T(8,128)S(1)} %get-tuple-element.12) | data formatting | bytes 12582912
  150.8 0.6 copy.9
  151.4 0.6 copy.10
Async XLA Ops:
  0.6 1.9 %copy-start = (bf16[2048,768]{1,0:T(8,128)(2,1)S(1)}, bf16[2048,768]{1,0:T(8,128)(2,1)}, u32[]{:S(2)}) copy-start(bf16[2048,768]{1,0:T(8,128)(2,1)} %c_ref.1) | copy-start | bytes 9437188
  2.5 1.4 copy-start.1
